TPU v7x, 32 devices: a whole 2x2x4 slice. The times are simulated.
32 devices in a mesh: rep: 4 (over y, core), ep: 8 (over z, x).
Axes of the slice: x: 2, y: 2, z: 4, core: 2. Of those that a mesh axis runs over, the one named last changes fastest.
Arguments:
- tokens: bfloat16 [24576, 2048], P(('rep', 'ep')), may hold values from -6 to 6
- route: int32 [2, 16384], P(None, ('rep', 'ep')), may hold values from 0 to 767, as said below
- cotangent: bfloat16 [2, 16384, 512], P(None, ('rep', 'ep')), may hold values from -6 to 6
- weight: float32 [2, 2048, 512], P(None, 'ep'), may hold values from -0.125 to 0.125
- first_q: int32 [2, 2048, 512], P(None, 'ep'), may hold values from -127 to 127
- first_scale: float32 [2, 2048, 4], P(None, 'ep'), may hold values from 3e-05 to 6e-05
- second_q: int32 [2, 2048, 512], P(None, 'ep'), may hold values from 32 to 127
- second_scale: float32 [2, 2048, 4], P(None, 'ep'), may hold values from 3e-09 to 8e-09
Outputs:
- token_grad: bfloat16 [24576, 2048], P(('rep', 'ep'))
- step_dir: float32 [2, 2048, 512], P(None, 'ep')
- new_weight: float32 [2, 2048, 512], P(None, 'ep')
- next_gate: bfloat16 [2, 16384, 512], P(None, ('rep', 'ep'))
Inputs may be any that keep to these rules, and one draw needn't show every extreme that they name: `route`: for each hot expert, the 512 entries of one device's rows (aligned blocks of 512 along the last dimension) are distinct.
All inputs are finite; a program needn't handle non-finite values.
Results may differ from a plain program's by a relative error of at most 0.006.
Values may be sent and summed in bfloat16 or wider, within the bound.
A program may use at most 128 MiB of HBM per device.

v0:
```python
import jax
import jax.numpy as jnp
from jax import lax
from jax.sharding import PartitionSpec as P

QBLOCK = 128


BETA_ONE = 0.9
BETA_TWO = 0.95
CORR_ONE = 1.0 - 0.9**10
CORR_TWO = 1.0 - 0.95**10
EPSILON = 1e-08
RATE = 0.002


def dequant(quant, scale):
    shaped = quant.astype(jnp.float32).reshape(quant.shape[0], quant.shape[1], -1, QBLOCK)
    return (shaped * scale[..., None]).reshape(quant.shape)


def adam_update(weight, grad, first_q, first_scale, second_q, second_scale):
    first = BETA_ONE * dequant(first_q, first_scale) + (1.0 - BETA_ONE) * grad
    second = BETA_TWO * dequant(second_q, second_scale) + (1.0 - BETA_TWO) * grad * grad
    step = first / CORR_ONE / (jnp.sqrt(second / CORR_TWO) + EPSILON)
    return (step, weight - RATE * step)


def owned_slice(array, offset, length):
    return lax.dynamic_slice_in_dim(array, offset, length, 1)


def on_device(tokens, route, cotangent, weight, first_q, first_scale, second_q, second_scale):
    n_rep = lax.axis_size("rep")
    n_ep = lax.axis_size("ep")
    experts, rows_here = route.shape
    width = tokens.shape[1]
    feature = cotangent.shape[2]
    total_rows = rows_here * n_rep * n_ep
    chosen = tokens[route]
    whole = lax.all_gather(weight.astype(jnp.bfloat16), "ep", axis=1, tiled=True)
    gate = jnp.einsum("erd,edf->erf", chosen, whole, preferred_element_type=jnp.float32)
    sig = jax.nn.sigmoid(gate)
    dgate = (cotangent.astype(jnp.float32) * sig * (1.0 + gate * (1.0 - sig))).astype(jnp.bfloat16)
    dx = jnp.einsum("erf,edf->erd", dgate, whole, preferred_element_type=jnp.float32)
    token_grad = (
        jnp.zeros(tokens.shape, jnp.float32)
        .at[route.reshape(-1)]
        .add(dx.reshape(-1, width))
        .astype(jnp.bfloat16)
    )
    owned = weight.shape[1]
    piece = owned // n_rep
    shuffled = (
        chosen.reshape(experts, rows_here, n_ep, n_rep, piece)
        .transpose(0, 1, 3, 2, 4)
        .reshape(experts, rows_here, width)
    )
    columns = shuffled
    quarter = lax.psum_scatter(
        jnp.einsum("erd,erf->def", columns, dgate, preferred_element_type=jnp.float32).reshape(
            lax.axis_size("rep") * (width // n_rep), experts * feature
        ),
        "rep",
        scatter_dimension=0,
        tiled=True,
    )
    summed = lax.psum_scatter(quarter, "ep", scatter_dimension=0, tiled=True)
    grad = summed.reshape(piece, experts, feature).transpose(1, 0, 2) / total_rows
    offset = lax.axis_index("rep") * piece
    step_part, weight_part = adam_update(
        owned_slice(weight, offset, piece),
        grad,
        owned_slice(first_q, offset, piece),
        owned_slice(first_scale, offset, piece),
        owned_slice(second_q, offset, piece),
        owned_slice(second_scale, offset, piece),
    )
    step_dir, new_weight = (
        lax.all_gather(step_part, "rep", axis=1, tiled=True),
        lax.all_gather(weight_part, "rep", axis=1, tiled=True),
    )
    columns = chosen
    next_gate = jnp.einsum(
        "erd,edf->erf",
        columns,
        lax.all_gather(new_weight.astype(jnp.bfloat16), "ep", axis=1, tiled=True),
        preferred_element_type=jnp.float32,
    ).astype(jnp.bfloat16)
    return (token_grad, step_dir, new_weight, next_gate)


def solution(mesh):
    in_specs = (
        P(("rep", "ep"), None),
        P(None, ("rep", "ep")),
        P(None, ("rep", "ep"), None),
        P(None, "ep", None),
        P(None, "ep", None),
        P(None, "ep", None),
        P(None, "ep", None),
        P(None, "ep", None),
    )
    out_specs = (
        P(("rep", "ep"), None),
        P(None, "ep", None),
        P(None, "ep", None),
        P(None, ("rep", "ep"), None),
    )
    return jax.shard_map(
        on_device, mesh=mesh, in_specs=in_specs, out_specs=out_specs, check_vma=False
    )
```

profile of v0, /device:TPU:0, one launch (start us, length us, event | category | flops | bytes accessed | tf_op | source)
XLA Modules:
  0.0 380.0 jit_solution(1324557947575599706)
XLA Ops:
  7.2 2.2 convert_element_type.25
  9.5 0.7 fusion.9
  10.2 6.0 %gather_fusion = bf16[1024,2048]{1,0:T(8,128)(2,1)} fusion(bf16[768,2048]{1,0:T(8,128)(2,1)S(1)} %copy-done, s32[1024]{0:T(1024)S(1)} %broadcast_clamp_fusion), kind=kCustom, calls=%fused_computation | custom fusion | bytes 8392704 | tf_op jit(solution)/shard_map/gather | solution.py:40
  16.2 6.5 %copy.17 = bf16[1024,2048]{0,1:T(8,128)(2,1)} copy(bf16[1024,2048]{1,0:T(8,128)(2,1)} %gather_fusion) | data formatting | bytes 8388608 | tf_op jit(solution)/shard_map/gather | solution.py:40
  22.7 7.8 %reshape.69 = bf16[2,512,8,4,64]{1,0,4,3,2:T(2,128)(2,1)} reshape(bf16[1024,2048]{0,1:T(8,128)(2,1)} %copy.17) | data formatting | bytes 8388608 | tf_op jit(solution)/shard_map/reshape | solution.py:55
  30.5 5.2 %copy.18 = bf16[2,512,4,8,64]{1,4,3,2,0:T(8,128)(2,1)} copy(bf16[2,512,4,8,64]{1,0,4,2,3:T(2,128)(2,1)} %bitcast.71) | data formatting | bytes 8388608 | tf_op jit(solution)/shard_map/transpose | solution.py:56
  35.7 50.6 %all-gather.5.cloned.1.call-done = bf16[2,2048,512]{2,1,0:T(8,128)(2,1)} async-done(((bf16[2,256,512]{2,1,0:T(8,128)(2,1)}), bf16[2,2048,512]{2,1,0:T(8,128)(2,1)}) %all-gather.5.cloned.1.call-update) | async-done | bytes 4194320 | tf_op jit(solution)/shard_map/all_gather | solution.py:41
  86.3 5.9 %fusion.13 = f32[2,512,512]{2,1,0:T(8,128)S(1)} fusion(bf16[2,512,2048]{2,1,0:T(8,128)(2,1)} %bitcast.69, bf16[2,2048,512]{2,1,0:T(8,128)(2,1)} %all-gather.5.cloned.1.call-done), kind=kOutput, calls=%fused_computation.26 | convolution fusion | flops 2147483648 | bytes 10485760 | tf_op jit(solution)/shard_map/erd,edf->erf/dot_general | solution.py:42
  92.2 6.3 %fusion.10 = f32[2,512,2048]{2,1,0:T(8,128)} fusion(bf16[2,512,2048]{1,2,0:T(8,128)(2,1)S(1)} %bitcast.73, f32[2,512,512]{2,1,0:T(8,128)S(1)} %fusion.13, bf16[2,512,512]{2,1,0:T(8,128)(2,1)S(1)} %copy-done.7), kind=kOutput, calls=%fused_computation.24 | convolution fusion | flops 2152726528 | bytes 15728640 | tf_op jit(solution)/shard_map/erd,erf->def/dot_general | solution.py:61
  98.5 9.3 %copy.21 = f32[2048,1024]{1,0:T(8,128)} copy(f32[2048,1024]{0,1:T(8,128)} %bitcast.72) | data formatting | bytes 16777216 | tf_op jit(solution)/shard_map/reshape | solution.py:61
  107.9 70.0 %reduce-scatter.3.cloned.1.call-done = f32[512,1024]{1,0:T(8,128)} async-done(((f32[2048,1024]{1,0:T(8,128)}), f32[512,1024]{1,0:T(8,128)}) %reduce-scatter.3.cloned.1.call-update) | async-done | bytes 2097168 | tf_op jit(solution)/shard_map/reduce_scatter | solution.py:60
  179.0 70.9 %reduce-scatter.5.cloned.1.call-done = f32[64,1024]{1,0:T(8,128)} async-done(((f32[512,1024]{1,0:T(8,128)}), f32[64,1024]{1,0:T(8,128)}) %reduce-scatter.5.cloned.1.call-update) | async-done | bytes 262160 | tf_op jit(solution)/shard_map/reduce_scatter | solution.py:68
  249.9 1.0 broadcast_multiply_fusion
  250.9 2.1 multiply_subtract_fusion
  253.1 0.5 all-gather.7.cloned.1.call-update
  253.8 15.1 %all-gather.9.cloned.1.call-done = f32[2,256,512]{2,1,0:T(8,128)} async-done(((f32[2,64,512]{2,1,0:T(8,128)}), f32[2,256,512]{2,1,0:T(8,128)}) %all-gather.9.cloned.1.call-update) | async-done | bytes 1048592 | tf_op jit(solution)/shard_map/all_gather | solution.py:81
  268.9 2.1 convert_element_type.30
  271.1 8.8 %fusion.11 = f32[2,512,2048]{2,1,0:T(8,128)} fusion(bf16[2,2048,512]{2,1,0:T(8,128)(2,1)} %all-gather.5.cloned.1.call-done, f32[2,512,512]{2,1,0:T(8,128)} %copy-done.8, bf16[2,512,512]{2,1,0:T(8,128)(2,1)S(1)} %copy-done.7), kind=kOutput, calls=%fused_computation.25 | convolution fusion | flops 2152726528 | bytes 15728640 | tf_op jit(solution)/shard_map/erf,edf->erd/dot_general | solution.py:45
  279.9 17.8 %scatter_custom_fusion = f32[768,2048]{1,0:T(8,128)} fusion(s32[1024]{0:T(1024)S(1)} %bitcast.79, f32[1024,2048]{1,0:T(8,128)} %bitcast.80, f32[]{:T(128)} %constant.16.clone.1), kind=kCustom, calls=%fused_computation.2 | custom fusion | flops 2097152 | bytes 6291968 | tf_op jit(solution)/shard_map/scatter-add | solution.py:49
  297.7 5.2 %convert_element_type.27 = bf16[768,2048]{1,0:T(8,128)(2,1)} convert(f32[768,2048]{1,0:T(8,128)} %scatter_custom_fusion) | non-fusion elementwise | flops 1572864 | bytes 9437184 | tf_op jit(solution)/shard_map/convert_element_type | solution.py:50
  302.9 60.2 %all-gather.11.cloned.1.call-done = bf16[2,2048,512]{2,1,0:T(8,128)(2,1)} async-done(((bf16[2,256,512]{2,1,0:T(8,128)(2,1)}), bf16[2,2048,512]{2,1,0:T(8,128)(2,1)}) %all-gather.11.cloned.1.call-update) | async-done | bytes 4194320 | tf_op jit(solution)/shard_map/all_gather | solution.py:87
  363.1 6.9 %convolution_convert_fusion = bf16[2,512,512]{2,1,0:T(8,128)(2,1)} fusion(bf16[2,512,2048]{2,1,0:T(8,128)(2,1)} %bitcast.70, bf16[2,2048,512]{2,1,0:T(8,128)(2,1)} %all-gather.11.cloned.1.call-done), kind=kOutput, calls=%fused_computation.5 | convolution fusion | flops 2148007936 | bytes 9437184 | tf_op jit(solution)/shard_map/erd,edf->erf/dot_general | solution.py:84
  370.0 1.0 copy.37
  370.9 2.3 copy.38
  (41 shorter events, 1.5 us)
Async XLA Ops:
  7.2 3.1 copy-start
  7.2 79.1 %all-gather.5.cloned.1.call-start = ((), (), s32[]{:S(2)}) async-start(), calls=%async_computation.2 | async-start | bytes 4718592 | tf_op jit(solution)/shard_map/all_gather | solution.py:41
  9.5 168.4 %reduce-scatter.3.cloned.1.call-start = ((), (), s32[]{:S(2)}) async-start(), calls=%async_computation.3 | async-start | bytes 10485760 | tf_op jit(solution)/shard_map/reduce_scatter | solution.py:60
  86.3 5.9 %copy-start.2 = (bf16[2,512,4,8,64]{1,4,3,2,0:T(8,128)(2,1)S(1)}, bf16[2,512,4,8,64]{1,4,3,2,0:T(8,128)(2,1)}, u32[]{:S(2)}) copy-start(bf16[2,512,4,8,64]{1,4,3,2,0:T(8,128)(2,1)} %copy.18) | copy-start | bytes 12582916
  86.3 6.0 %copy-start.7 = (bf16[2,512,512]{2,1,0:T(8,128)(2,1)S(1)}, bf16[2,512,512]{2,1,0:T(8,128)(2,1)}, u32[]{:S(2)}) copy-start(bf16[2,512,512]{2,1,0:T(8,128)(2,1)} %param.10) | copy-start | bytes 3145732
  92.2 6.3 %copy-start.8 = (f32[2,512,512]{2,1,0:T(8,128)}, f32[2,512,512]{2,1,0:T(8,128)S(1)}, u32[]{:S(2)}) copy-start(f32[2,512,512]{2,1,0:T(8,128)S(1)} %fusion.13) | copy-start | bytes 6291460
  107.8 70.2 %copy-start.5 = (f32[2,256,4]{1,2,0:T(4,128)S(1)}, f32[2,256,4]{1,2,0:T(4,128)}, u32[]{:S(2)}) copy-start(f32[2,256,4]{1,2,0:T(4,128)} %param.15) | copy-start | bytes 24580
  107.8 70.2 %copy-start.6 = (f32[2,256,4]{1,2,0:T(4,128)S(1)}, f32[2,256,4]{1,2,0:T(4,128)}, u32[]{:S(2)}) copy-start(f32[2,256,4]{1,2,0:T(4,128)} %param.13) | copy-start | bytes 24580
  107.8 142.0 %reduce-scatter.5.cloned.1.call-start = ((), (), s32[]{:S(2)}) async-start(), calls=%async_computation.4 | async-start | bytes 2359296 | tf_op jit(solution)/shard_map/reduce_scatter | solution.py:68
  178.0 93.1 %copy-start.4 = (s32[2,512]{1,0:T(2,128)S(1)}, s32[2,512]{1,0:T(2,128)}, u32[]{:S(2)}) copy-start(s32[2,512]{1,0:T(2,128)} %param.9) | copy-start | bytes 12292
  178.0 91.0 %all-gather.9.cloned.1.call-start = ((), (), s32[]{:S(2)}) async-start(), calls=%async_computation.6 | async-start | bytes 1310720 | tf_op jit(solution)/shard_map/all_gather | solution.py:81
  253.0 49.8 %all-gather.7.cloned.1.call-start = ((), (), s32[]{:S(2)}) async-start(), calls=%async_computation.5 | async-start | bytes 1310720 | tf_op jit(solution)/shard_map/all_gather | solution.py:80
  253.6 109.4 %all-gather.11.cloned.1.call-start = ((), (), s32[]{:S(2)}) async-start(), calls=%async_computation.7 | async-start | bytes 4718592 | tf_op jit(solution)/shard_map/all_gather | solution.py:87
  363.1 6.9 %copy-start.3 = (f32[2,256,512]{2,1,0:T(8,128)S(1)}, f32[2,256,512]{2,1,0:T(8,128)}, u32[]{:S(2)}) copy-start(f32[2,256,512]{2,1,0:T(8,128)} %all-gather.7.cloned.1.call-done) | copy-start | bytes 3145732
  363.1 10.1 %copy-start.1 = (bf16[768,2048]{1,0:T(8,128)(2,1)S(1)}, bf16[768,2048]{1,0:T(8,128)(2,1)}, u32[]{:S(2)}) copy-start(bf16[768,2048]{1,0:T(8,128)(2,1)} %param.8) | copy-start | bytes 9437188
Sparse Core Ops, SparseCore 0:
  10.7 75.4 all-gather.4
  108.0 69.9 reduce-scatter.2
  181.5 68.3 reduce-scatter.4
  253.2 15.7 all-gather.8
  270.9 16.6 all-gather.6
  290.3 72.7 all-gather.10
where the time goes:
time: 381 us; the launch traced here: 380 us
  waiting for transfers between devices  267 us (70%)
  local copies, waits for them, and re-layouts  38.9 us (10%)
  other arithmetic  31.1 us (8%)
  matrix products  27.9 us (7%)
  between operations  14.3 us (4%)
    reduce_scatter x1, waiting for transfers between devices, on_device(): summed = lax.psum_scatter(quarter, 'ep', scatter_dimension=0, tiled=True)  70.9 us
    reduce_scatter x1, waiting for transfers between devices, on_device(): lax.psum_scatter(jnp.einsum('erd,erf->def', columns, dgate, preferred_ele...  70 us
    all_gather x1, waiting for transfers between devices, on_device(): lax.all_gather(new_weight.astype(jnp.bfloat16), 'ep', axis=1, tiled=True)  60.2 us
    all_gather x1, waiting for transfers between devices, on_device(): lax.all_gather(weight.astype(jnp.bfloat16), 'ep', axis=1, tiled=True)  50.6 us
    scatter-add x1, other arithmetic, on_device(): token_grad = jnp.zeros(tokens.shape, jnp.float32).at[route.reshape(-1)].a...  17.8 us
    all_gather x1, waiting for transfers between devices, on_device(): lax.all_gather(weight_part, 'rep', axis=1, tiled=True)  15.1 us
    gather x2, local copies, waits for them, and re-layouts, on_device(): chosen = tokens[route]  12.5 us
    reshape x1, local copies, waits for them, and re-layouts, on_device(): jnp.einsum('erd,erf->def', columns, dgate, preferred_element_type=jnp.flo...  9.3 us
  transfers between devices with their start and end apart: 6, of which 5 were waited for; matrix products, arithmetic and copies ran while one was open for 16% of the time, Pallas kernels for 0%

commit v1 on v0

v1 whole, which is shorter than its diff:
```python
import jax
import jax.numpy as jnp
from jax import lax
from jax.sharding import PartitionSpec as P

QBLOCK = 128
BETA_ONE = 0.9
BETA_TWO = 0.95
CORR_ONE = 1.0 - 0.9**10
CORR_TWO = 1.0 - 0.95**10
EPSILON = 1e-08
RATE = 0.002
BF = jnp.bfloat16
F32 = jnp.float32


def dequant(quant, scale):
    shaped = quant.astype(F32).reshape(quant.shape[0], quant.shape[1], -1, QBLOCK)
    return (shaped * scale[..., None]).reshape(quant.shape)


def adam_update(weight, grad, first_q, first_scale, second_q, second_scale):
    first = BETA_ONE * dequant(first_q, first_scale) + (1.0 - BETA_ONE) * grad
    second = BETA_TWO * dequant(second_q, second_scale) + (1.0 - BETA_TWO) * grad * grad
    step = first / CORR_ONE / (jnp.sqrt(second / CORR_TWO) + EPSILON)
    return (step, weight - RATE * step)


def on_device(tokens, route, cotangent, weight, first_q, first_scale, second_q, second_scale):
    n_rep = lax.axis_size("rep")
    n_ep = lax.axis_size("ep")
    experts, rows_here = route.shape
    count, width = tokens.shape
    feature = cotangent.shape[2]
    owned = weight.shape[1]
    piece = owned // n_rep
    total_rows = rows_here * n_rep * n_ep
    whole = lax.all_gather(weight.astype(BF), "ep", axis=1, tiled=True)
    spots = lax.broadcasted_iota(jnp.int32, (experts, count, rows_here), 1)
    pick = (spots == route[:, None, :]).astype(BF)
    cot = jnp.einsum("etr,erf->etf", pick, cotangent, preferred_element_type=F32)
    gate = jnp.einsum("td,edf->etf", tokens, whole, preferred_element_type=F32)
    sig = jax.nn.sigmoid(gate)
    dgate = (cot * sig * (1.0 + gate * (1.0 - sig))).astype(BF)
    partial = jnp.einsum("td,etf->edf", tokens, dgate, preferred_element_type=F32).astype(BF)
    shuffled = (
        partial.reshape(experts, n_ep, n_rep, piece, feature)
        .transpose(2, 1, 3, 0, 4)
        .reshape(n_rep * n_ep * piece, experts * feature)
    )
    quarter = lax.psum_scatter(shuffled, "rep", scatter_dimension=0, tiled=True)
    summed = lax.psum_scatter(quarter, "ep", scatter_dimension=0, tiled=True)
    token_grad = jnp.einsum("etf,edf->td", dgate, whole, preferred_element_type=F32).astype(BF)
    grad = lax.all_gather(summed, "rep", axis=0, tiled=True).astype(F32)
    grad = grad.reshape(owned, experts, feature).transpose(1, 0, 2) / total_rows
    step_dir, new_weight = adam_update(
        weight, grad, first_q, first_scale, second_q, second_scale
    )
    new_whole = lax.all_gather(new_weight.astype(BF), "ep", axis=1, tiled=True)
    nexts = jnp.einsum("td,edf->etf", tokens, new_whole, preferred_element_type=F32).astype(BF)
    next_gate = jnp.einsum("etr,etf->erf", pick, nexts, preferred_element_type=F32).astype(BF)
    return (token_grad, step_dir, new_weight, next_gate)


def solution(mesh):
    in_specs = (
        P(("rep", "ep"), None),
        P(None, ("rep", "ep")),
        P(None, ("rep", "ep"), None),
        P(None, "ep", None),
        P(None, "ep", None),
        P(None, "ep", None),
        P(None, "ep", None),
        P(None, "ep", None),
    )
    out_specs = (
        P(("rep", "ep"), None),
        P(None, "ep", None),
        P(None, "ep", None),
        P(None, ("rep", "ep"), None),
    )
    return jax.shard_map(
        on_device, mesh=mesh, in_specs=in_specs, out_specs=out_specs, check_vma=False
    )
```

time: 381 us -> 341 us (0.90)
  waiting for transfers between devices: 267 us -> 239 us
  other arithmetic: 31.1 us -> 8.46 us
  blocking collectives: 0 us -> 7.38 us
  matrix products: 27.9 us -> 32.7 us
    reduce_scatter x1, waiting for transfers between devices: 70 us -> 42.9 us  [on_device(): quarter = lax.psum_scatter(shuffled, 'rep', scatter_dimension=0, tiled=True)]
    scatter-add x1 -> x0, other arithmetic: 17.8 us -> none  [on_device(): token_grad = jnp.zeros(tokens.shape, jnp.float32).at[route.reshape(-1)].a...]
    reshape x2 -> x0, local copies, waits for them, and re-layouts: 17.1 us -> none  [the longest x1 9.3 us: on_device(): jnp.einsum('erd,erf->def', columns, dgate, preferred_element_type=jnp.flo...]
    unnamed x22 -> x16, local copies, waits for them, and re-layouts: 3.29 us -> 19.4 us
    gather x2 -> x0, local copies, waits for them, and re-layouts: 12.5 us -> none  [on_device(): chosen = tokens[route]]
    reduce_scatter x1, waiting for transfers between devices: 70.9 us -> 62.2 us  [on_device(): summed = lax.psum_scatter(quarter, 'ep', scatter_dimension=0, tiled=True)]
    all_gather x4 -> x2, waiting for transfers between devices: 126 us -> 133 us  [the longest x1 73.3 us: on_device(): whole = lax.all_gather(weight.astype(BF), 'ep', axis=1, tiled=True)]
    all_gather x0 -> x1, blocking collectives: none -> 7.38 us  [on_device(): grad = lax.all_gather(summed, 'rep', axis=0, tiled=True).astype(F32)]
  transfers between devices with their start and end apart: 6 -> 4, of which waited for: 5 -> 4; matrix products, arithmetic and copies ran while one was open for 16% -> 6% of each run, Pallas kernels for 0% -> 0%
where the time goes in v1:
time: 341 us
  waiting for transfers between devices  239 us (70%)
  local copies, waits for them, and re-layouts  39.2 us (11%)
  matrix products  32.7 us (10%)
  between operations  13.8 us (4%)
  other arithmetic  8.46 us (2%)
  blocking collectives  7.38 us (2%)
    all_gather x1, waiting for transfers between devices, on_device(): whole = lax.all_gather(weight.astype(BF), 'ep', axis=1, tiled=True)  73.3 us
    reduce_scatter x1, waiting for transfers between devices, on_device(): summed = lax.psum_scatter(quarter, 'ep', scatter_dimension=0, tiled=True)  62.2 us
    all_gather x1, waiting for transfers between devices, on_device(): new_whole = lax.all_gather(new_weight.astype(BF), 'ep', axis=1, tiled=True)  60.2 us
    reduce_scatter x1, waiting for transfers between devices, on_device(): quarter = lax.psum_scatter(shuffled, 'rep', scatter_dimension=0, tiled=True)  42.9 us
    unnamed x16, local copies, waits for them, and re-layouts  19.4 us
    dot_general x1, matrix products, on_device(): jnp.einsum('etr,etf->erf', pick, nexts, preferred_element_type=F32)  8.67 us
    transpose x1, local copies, waits for them, and re-layouts, on_device(): shuffled = partial.reshape(experts, n_ep, n_rep, piece, feature).transpos...  8.51 us
    dot_general x1, matrix products, on_device(): jnp.einsum('etf,edf->td', dgate, whole, preferred_element_type=F32)  7.75 us
  transfers between devices with their start and end apart: 4, of which 4 were waited for; matrix products, arithmetic and copies ran while one was open for 6% of the time, Pallas kernels for 0%

profile of v1, /device:TPU:0, one launch (start us, length us, event | category | flops | bytes accessed | tf_op | source)
XLA Modules:
  0.0 340.5 jit_solution(5736944138248286152)
XLA Ops:
  7.2 2.7 copy.20
  9.9 2.1 convert_element_type.35
  12.1 4.2 %fusion.12 = f32[2,768,512]{2,1,0:T(8,128)} fusion(bf16[2,512,512]{2,1,0:T(8,128)(2,1)} %param.10, s32[2,512]{1,0:T(2,128)S(1)} %copy-done.3), kind=kOutput, calls=%fused_computation.17 | convolution fusion | flops 806092800 | bytes 4198400 | tf_op jit(solution)/shard_map/etr,erf->etf/dot_general | solution.py:41
  16.3 73.3 %all-gather.3.cloned.1.call-done = bf16[2,2048,512]{1,2,0:T(8,128)(2,1)} async-done(((bf16[2,256,512]{1,2,0:T(8,128)(2,1)}), bf16[2,2048,512]{1,2,0:T(8,128)(2,1)}) %all-gather.3.cloned.1.call-update) | async-done | bytes 4194320 | tf_op jit(solution)/shard_map/all_gather | solution.py:38
  89.5 7.1 %fusion.5 = bf16[2,768,512]{2,1,0:T(8,128)(2,1)S(1)} fusion(f32[2,768,512]{2,1,0:T(8,128)} %fusion.12, bf16[2,2048,512]{1,2,0:T(8,128)(2,1)} %all-gather.3.cloned.1.call-done, bf16[768,2048]{1,0:T(8,128)(2,1)S(1)} %copy-done), kind=kOutput, calls=%fused_computation.9 | convolution fusion | flops 3228303360 | bytes 12058624 | tf_op jit(solution)/shard_map/td,edf->etf/dot_general | solution.py:42
  96.6 1.2 copy-done.4
  97.8 5.0 %convert_bitcast_fusion = bf16[2,2048,512]{1,2,0:T(8,128)(2,1)} fusion(bf16[2,768,512]{2,1,0:T(8,128)(2,1)S(1)} %fusion.5, bf16[768,2048]{1,0:T(8,128)(2,1)S(1)} %copy-done), kind=kOutput, calls=%fused_computation.1 | convolution fusion | flops 3223322624 | bytes 8912896 | tf_op jit(solution)/shard_map/td,etf->edf/dot_general | solution.py:45
  102.8 6.2 %copy.25 = bf16[2,2048,512]{2,1,0:T(8,128)(2,1)} copy(bf16[2,2048,512]{1,2,0:T(8,128)(2,1)} %convert_bitcast_fusion) | data formatting | bytes 8388608 | tf_op jit(solution)/shard_map/convert_element_type | solution.py:45
  109.1 8.5 %copy.26 = bf16[4,8,64,2,512]{4,3,2,1,0:T(2,128)(2,1)} copy(bf16[4,8,64,2,512]{4,2,0,1,3:T(8,128)(2,1)} %bitcast.79) | data formatting | bytes 8388608 | tf_op jit(solution)/shard_map/transpose | solution.py:48
  117.6 5.4 %copy.37 = bf16[256,8,2,512]{3,1,2,0:T(8,128)(2,1)} copy(bf16[256,8,2,512]{3,2,1,0:T(2,128)(2,1)} %bitcast.80) | data formatting | bytes 8388608
  123.0 42.9 %reduce-scatter.3.cloned.1.call-done = bf16[512,1024]{1,0:T(8,128)(2,1)} async-done(((bf16[2048,1024]{1,0:T(8,128)(2,1)}), bf16[512,1024]{1,0:T(8,128)(2,1)}) %reduce-scatter.3.cloned.1.call-update) | async-done | bytes 1048592 | tf_op jit(solution)/shard_map/reduce_scatter | solution.py:51
  166.1 2.5 copy.28
  168.6 2.6 copy.23
  171.2 62.2 %reduce-scatter.5.cloned.1.call-done = bf16[64,1024]{1,0:T(8,128)(2,1)} async-done(((bf16[512,1024]{1,0:T(8,128)(2,1)}), bf16[64,1024]{1,0:T(8,128)(2,1)}) %reduce-scatter.5.cloned.1.call-update) | async-done | bytes 131088 | tf_op jit(solution)/shard_map/reduce_scatter | solution.py:52
  233.4 7.4 %all_gather.10 = bf16[256,1024]{1,0:T(8,128)(2,1)S(1)} all-gather(bf16[64,1024]{1,0:T(8,128)(2,1)} %reduce-scatter.5.cloned.1.call-done), channel_id=1, replica_groups=mesh['rep'=4,'ep'=8] {'rep'}, dimensions={0}, use_global_device_ids=true | all-gather | bytes 655360 | tf_op jit(solution)/shard_map/all_gather | solution.py:54
  240.8 1.6 convert_multiply_fusion.2
  242.4 2.5 copy.29
  244.9 2.5 copy.27
  247.4 4.8 %fusion.33 = (bf16[2,256,512]{1,2,0:T(8,128)(2,1)}, f32[2,256,512]{1,2,0:T(8,128)}, f32[2,256,512]{1,2,0:T(8,128)}) fusion(f32[2,256,512]{1,2,0:T(8,128)} %copy.20, f32[2,256,512]{1,2,0:T(8,128)} %bitcast.81, f32[2,256,4]{1,2,0:T(4,128)S(1)} %copy-done.1, s32[2,256,512]{1,2,0:T(8,128)} %copy.28, f32[2,256,512]{1,2,0:T(8,128)} %bitcast.82, ...), kind=kLoop, calls=%fused_computation.38 | loop fusion | flops 3932160 | bytes 7880704 | tf_op jit(solution)/shard_map/convert_element_type | solution.py:59
  252.2 7.7 %bitcast_convert_fusion = bf16[768,2048]{1,0:T(8,128)(2,1)} fusion(bf16[2,768,512]{2,1,0:T(8,128)(2,1)} %copy-done.4, bf16[2,2048,512]{1,2,0:T(8,128)(2,1)} %all-gather.3.cloned.1.call-done), kind=kOutput, calls=%fused_computation | convolution fusion | flops 3222798336 | bytes 8912896 | tf_op jit(solution)/shard_map/etf,edf->td/dot_general | solution.py:53
  260.0 2.6 copy.31
  262.5 2.5 copy.32
  265.1 60.2 %all-gather.5.cloned.1.call-done = bf16[2,2048,512]{1,2,0:T(8,128)(2,1)} async-done(((bf16[2,256,512]{1,2,0:T(8,128)(2,1)}), bf16[2,2048,512]{1,2,0:T(8,128)(2,1)}) %all-gather.5.cloned.1.call-update) | async-done | bytes 4194320 | tf_op jit(solution)/shard_map/all_gather | solution.py:59
  325.3 8.7 %fusion.20 = bf16[2,512,512]{2,1,0:T(8,128)(2,1)} fusion(s32[2,512]{1,0:T(2,128)S(1)} %copy-done.3, bf16[2,2048,512]{1,2,0:T(8,128)(2,1)} %all-gather.5.cloned.1.call-done, bf16[768,2048]{1,0:T(8,128)(2,1)S(1)} %copy-done), kind=kOutput, calls=%fused_computation.24 | convolution fusion | flops 4028628992 | bytes 8392704 | tf_op jit(solution)/shard_map/etr,etf->erf/dot_general | solution.py:61
  (17 shorter events, 0.4 us)
Async XLA Ops:
  7.2 82.4 %copy-start = (bf16[768,2048]{1,0:T(8,128)(2,1)S(1)}, bf16[768,2048]{1,0:T(8,128)(2,1)}, u32[]{:S(2)}) copy-start(bf16[768,2048]{1,0:T(8,128)(2,1)} %param.8) | copy-start | bytes 9437188
  7.2 4.9 %copy-start.3 = (s32[2,512]{1,0:T(2,128)S(1)}, s32[2,512]{1,0:T(2,128)}, u32[]{:S(2)}) copy-start(s32[2,512]{1,0:T(2,128)} %param.9) | copy-start | bytes 12292
  7.2 82.3 %all-gather.3.cloned.1.call-start = ((), (), s32[]{:S(2)}) async-start(), calls=%async_computation.2 | async-start | bytes 4718592 | tf_op jit(solution)/shard_map/all_gather | solution.py:38
  12.0 153.9 %reduce-scatter.3.cloned.1.call-start = ((), (), s32[]{:S(2)}) async-start(), calls=%async_computation.3 | async-start | bytes 5242880 | tf_op jit(solution)/shard_map/reduce_scatter | solution.py:51
  96.6 1.2 copy-start.4
  123.0 110.4 %reduce-scatter.5.cloned.1.call-start = ((), (), s32[]{:S(2)}) async-start(), calls=%async_computation.4 | async-start | bytes 1179648 | tf_op jit(solution)/shard_map/reduce_scatter | solution.py:52
  165.9 159.4 %all-gather.5.cloned.1.call-start = ((), (), s32[]{:S(2)}) async-start(), calls=%async_computation.5 | async-start | bytes 4718592 | tf_op jit(solution)/shard_map/all_gather | solution.py:59
  240.8 6.7 %copy-start.1 = (f32[2,256,4]{1,2,0:T(4,128)S(1)}, f32[2,256,4]{1,2,0:T(4,128)}, u32[]{:S(2)}) copy-start(f32[2,256,4]{1,2,0:T(4,128)} %param.15) | copy-start | bytes 24580
  240.8 6.7 %copy-start.2 = (f32[2,256,4]{1,2,0:T(4,128)S(1)}, f32[2,256,4]{1,2,0:T(4,128)}, u32[]{:S(2)}) copy-start(f32[2,256,4]{1,2,0:T(4,128)} %param.13) | copy-start | bytes 24580
Sparse Core Ops, SparseCore 0:
  12.1 77.3 all-gather.2
  123.1 42.7 reduce-scatter.2
  169.3 64.0 reduce-scatter.4
  252.4 72.8 all-gather.4

commit v2 on v1

--- a/solution.py
+++ b/solution.py
@@ -1,6 +1,10 @@
+import functools
+
 import jax
 import jax.numpy as jnp
 from jax import lax
+from jax.experimental import pallas as pl
+from jax.experimental.pallas import tpu as pltpu
 from jax.sharding import PartitionSpec as P
 
 QBLOCK = 128
@@ -13,6 +17,362 @@
 BF = jnp.bfloat16
 F32 = jnp.float32
 
+MESH = pl.DeviceIdType.MESH
+TILE = 16
+
+
+class Spot:
+    def __init__(self, n_ep, height):
+        self.rep, self.ep = lax.axis_index("rep"), lax.axis_index("ep")
+        self.core, self.y = self.rep % 2, self.rep // 2
+        self.x, self.z = self.ep % 2, self.ep // 2
+        self.n_ep, self.line, self.height = n_ep, n_ep // 2, height
+        self.alone = height // TILE * 3 // 8 * TILE
+        self.held = height - self.alone
+        self.both = self.held - self.alone
+        self.start = self.y * self.alone
+        self.x_peer = (self.rep, self.z * 2 + 1 - self.x)
+        self.y_peer = ((1 - self.y) * 2 + self.core, self.ep)
+        self.core_peer = (self.y * 2 + 1 - self.core, self.ep)
+        self.order = []
+        for k in range(1, self.line // 2 + 1):
+            self.order += [k] if k == self.line - k else [k, self.line - k]
+
+    def z_peer(self, k):
+        return (self.rep, (self.z + k) % self.line * 2 + self.x)
+
+    def meet(self):
+        barrier = pltpu.get_barrier_semaphore()
+        peers = [self.z_peer(k) for k in range(1, self.line)]
+        peers += [self.x_peer, self.y_peer, self.core_peer]
+        for peer in peers:
+            pl.semaphore_signal(barrier, inc=1, device_id=peer, device_id_type=MESH)
+        pl.semaphore_wait(barrier, len(peers))
+
+
+def tiled(value):
+    return pl.multiple_of(value, TILE)
+
+
+def remote(src, dst, send, recv, peer):
+    return pltpu.make_async_remote_copy(
+        src_ref=src, dst_ref=dst, send_sem=send, recv_sem=recv, device_id=peer, device_id_type=MESH
+    )
+
+
+class Gather:
+    def __init__(self, at, own, out, sems):
+        self.at, self.own, self.out = at, own, out
+        (self.zs, self.xs, self.ys, self.c1s, self.c2s, self.r1, self.r2, self.r3, self.r4) = sems
+        self.sent = []
+
+    def part(self, half, ep, first, rows):
+        return self.out.at[half, pl.ds(tiled(ep * self.at.height + first), rows)]
+
+    def mine(self, ep):
+        return self.part(self.at.core, ep, self.at.start, self.at.held)
+
+    def go(self, src, dst, send, recv, peer):
+        copy = remote(src, dst, send, recv, peer)
+        copy.start()
+        self.sent.append(copy)
+
+    def start(self):
+        at = self.at
+        at.meet()
+        src = self.own.at[at.core, pl.ds(tiled(at.start), at.held)]
+        for k in at.order:
+            self.go(src, self.mine(at.ep), self.zs.at[k], self.r1.at[at.ep], at.z_peer(k))
+        self.go(src, self.mine(at.ep), self.xs.at[0], self.r1.at[at.ep], at.x_peer)
+
+    def arrive(self, dst, recv):
+        at = self.at
+        remote(dst, dst, self.zs.at[0], recv, at.x_peer).wait_recv()
+
+    def share(self, ep):
+        at = self.at
+        if at.alone:
+            rows = self.part(at.core, ep, at.y * at.held, at.alone)
+            self.go(rows, rows, self.ys.at[ep], self.r2.at[ep], at.y_peer)
+        self.go(self.mine(ep), self.mine(ep), self.c1s.at[ep], self.r3.at[ep], at.core_peer)
+
+    def from_line(self, k):
+        at = self.at
+        ep = (at.z + at.line - k) % at.line * 2 + at.x
+        self.arrive(self.mine(ep), self.r1.at[ep])
+        self.go(self.mine(ep), self.mine(ep), self.xs.at[k], self.r1.at[ep], at.x_peer)
+        self.share(ep)
+
+    def from_pair(self, k):
+        at = self.at
+        ep = (at.z + at.line - k) % at.line * 2 + 1 - at.x
+        self.arrive(self.mine(ep), self.r1.at[ep])
+        self.share(ep)
+
+    def relay(self):
+        at = self.at
+        waiting = [0] + at.order
+        for k in at.order:
+            self.from_line(k)
+            self.from_pair(waiting.pop(0))
+        for k in waiting:
+            self.from_pair(k)
+        if at.alone:
+            for ep in self.others():
+                rows = self.part(at.core, ep, (1 - at.y) * at.held, at.alone)
+                self.arrive(rows, self.r2.at[ep])
+                self.go(rows, rows, self.c2s.at[ep], self.r4.at[ep], at.core_peer)
+
+    def others(self):
+        at = self.at
+        found = []
+        waiting = [0] + at.order
+        for k in at.order:
+            found.append((at.z + at.line - k) % at.line * 2 + at.x)
+            found.append((at.z + at.line - waiting.pop(0)) % at.line * 2 + 1 - at.x)
+        for k in waiting:
+            found.append((at.z + at.line - k) % at.line * 2 + 1 - at.x)
+        return found
+
+    def whole(self, ep):
+        at = self.at
+        self.arrive(self.part(1 - at.core, ep, at.start, at.held), self.r3.at[ep])
+        if at.alone:
+            self.arrive(
+                self.part(1 - at.core, ep, (1 - at.y) * at.held, at.alone), self.r4.at[ep]
+            )
+
+    def end(self):
+        for copy in self.sent:
+            copy.wait_send()
+
+
+def gather_sems(n_ep):
+    line = n_ep // 2
+    return [pltpu.SemaphoreType.DMA((line,)), pltpu.SemaphoreType.DMA((line,))] + [
+        pltpu.SemaphoreType.DMA((n_ep,)) for _ in range(7)
+    ]
+
+
+def gather_kernel(n_ep, own, out, *sems):
+    at = Spot(n_ep, own.shape[1])
+    job = Gather(at, own, out, sems)
+    job.start()
+    out[:, pl.ds(tiled(at.ep * at.height), at.height)] = own[...]
+    job.relay()
+    for ep in job.others():
+        job.whole(ep)
+    job.end()
+
+
+def gather_blocks(own, n_ep, tag):
+    halves, height, feature = own.shape
+    return pl.pallas_call(
+        functools.partial(gather_kernel, n_ep),
+        out_shape=jax.ShapeDtypeStruct((halves, n_ep * height, feature), own.dtype),
+        in_specs=[pl.BlockSpec(memory_space=pltpu.VMEM)],
+        out_specs=pl.BlockSpec(memory_space=pltpu.VMEM),
+        scratch_shapes=gather_sems(n_ep),
+        compiler_params=pltpu.CompilerParams(collective_id=tag, has_side_effects=True),
+        name=f"gather_{tag}",
+    )(own)
+
+
+class Reduce:
+    def __init__(self, at, inp, out, bufs, sems):
+        self.at, self.inp, self.out = at, inp, out
+        (self.bc, self.s1, self.by, self.s2, self.bx, self.bz, self.fin, self.by2) = bufs
+        (self.cs, self.cr, self.ys, self.yr, self.xs, self.xr, self.zs, self.zr, self.fs, self.fr) = sems
+
+    def block(self, i):
+        at = self.at
+        far = jnp.where(i < at.line, 1, 0)
+        z = (at.z + 1 + i) % at.line
+        x = at.x + far - 2 * at.x * far
+        return z, z * 2 + x
+
+    def core_copy(self, ep):
+        at = self.at
+        return remote(
+            self.inp.at[1 - at.core, pl.ds(tiled(ep * at.height), at.height)],
+            self.bc.at[ep],
+            self.cs.at[ep],
+            self.cr.at[ep],
+            at.core_peer,
+        )
+
+    def y_copy(self, ep):
+        at = self.at
+        return remote(
+            self.s1.at[ep, pl.ds(tiled((1 - at.y) * at.held), at.alone)],
+            self.by.at[ep],
+            self.ys.at[ep],
+            self.yr.at[ep],
+            at.y_peer,
+        )
+
+    def x_copy(self, z, ep):
+        return remote(self.s2.at[ep], self.bx.at[z], self.xs.at[z], self.xr.at[z], self.at.x_peer)
+
+    def z_copy(self, k, ep):
+        at = self.at
+        return remote(self.s2.at[ep], self.bz.at[k], self.zs.at[k], self.zr.at[k], at.z_peer(k))
+
+    def first(self, i):
+        at = self.at
+        _, ep = self.block(i)
+        self.core_copy(ep).wait_recv()
+        here = self.inp[at.core, pl.ds(tiled(ep * at.height), at.height)].astype(F32)
+        self.s1[ep] = (here + self.bc[ep].astype(F32)).astype(BF)
+        if at.alone:
+            self.y_copy(ep).start()
+
+    def pieces(self, ep):
+        at = self.at
+        found = []
+        if at.alone:
+            self.y_copy(ep).wait_recv()
+            value = self.s1[ep, pl.ds(tiled(at.y * at.held), at.alone)].astype(F32)
+            found.append((tiled(at.y * at.both), at.alone, value + self.by[ep].astype(F32)))
+        value = self.s1[ep, pl.ds(at.alone, at.both)].astype(F32)
+        found.append((tiled((1 - at.y) * at.alone), at.both, value))
+        return found
+
+    def second_far(self, i):
+        z, ep = self.block(i)
+        for first, rows, value in self.pieces(ep):
+            self.s2[ep, pl.ds(first, rows)] = value.astype(BF)
+        self.x_copy(z, ep).start()
+
+    def second_near(self, i):
+        z, ep = self.block(i)
+        found = self.pieces(ep)
+        self.x_copy(z, ep).wait_recv()
+        for first, rows, value in found:
+            total = value + self.bx[z, pl.ds(first, rows)].astype(F32)
+            self.s2[ep, pl.ds(first, rows)] = total.astype(BF)
+
+    def start(self):
+        at = self.at
+        at.meet()
+
+        @pl.loop(0, at.n_ep)
+        def _(i):
+            _, ep = self.block(i)
+            self.core_copy(ep).start()
+
+    def run(self, lag=3):
+        at = self.at
+        for i in range(min(lag, at.n_ep)):
+            self.first(i)
+
+        @pl.loop(0, at.line)
+        def _(i):
+            @pl.when(i + lag < at.n_ep)
+            def _():
+                self.first(i + lag)
+
+            self.second_far(i)
+
+        @pl.loop(at.line, at.n_ep - 1)
+        def _(i):
+            @pl.when(i + lag < at.n_ep)
+            def _():
+                self.first(i + lag)
+
+            self.second_near(i)
+            k = i - at.line + 1
+            _, ep = self.block(i)
+            self.z_copy(k, ep).start()
+
+        self.second_near(at.n_ep - 1)
+
+    def finish(self):
+        at = self.at
+        total = self.s2[at.ep].astype(F32)
+        for k in range(1, at.line):
+            self.z_copy(k, at.ep).wait_recv()
+            total += self.bz[k].astype(F32)
+        self.fin[...] = total.astype(BF)
+        swap = remote(self.fin, self.by2, self.fs.at[0], self.fr.at[0], at.y_peer)
+        swap.start()
+        half = self.out.at[at.core]
+        if at.alone:
+            half[pl.ds(tiled(at.y * at.held), at.alone)] = self.fin[
+                pl.ds(tiled(at.y * at.both), at.alone)
+            ]
+        swap.wait()
+        if at.alone:
+            half[pl.ds(tiled((1 - at.y) * at.held), at.alone)] = self.by2[
+                pl.ds(tiled((1 - at.y) * at.both), at.alone)
+            ]
+        here = self.fin[pl.ds(tiled((1 - at.y) * at.alone), at.both)].astype(F32)
+        there = self.by2[pl.ds(tiled(at.y * at.alone), at.both)].astype(F32)
+        half[pl.ds(at.alone, at.both)] = (here + there).astype(BF)
+        last = remote(half, half, self.fs.at[1], self.fr.at[1], at.core_peer)
+        last.start()
+        last.wait_send()
+        other = self.out.at[1 - at.core]
+        remote(other, other, self.fs.at[1], self.fr.at[1], at.core_peer).wait_recv()
+
+        @pl.loop(0, at.n_ep)
+        def _(i):
+            _, ep = self.block(i)
+            self.core_copy(ep).wait_send()
+            if at.alone:
+                self.y_copy(ep).wait_send()
+
+        @pl.loop(0, at.line)
+        def _(i):
+            z, ep = self.block(i)
+            self.x_copy(z, ep).wait_send()
+
+        @pl.loop(1, at.line)
+        def _(k):
+            self.z_copy(k, at.ep).wait_send()
+
+
+def reduce_bufs(n_ep, height, feature):
+    line = n_ep // 2
+    alone = height // TILE * 3 // 8 * TILE
+    held = height - alone
+    shapes = [
+        (n_ep, height),
+        (n_ep, height),
+        (n_ep, max(alone, TILE)),
+        (n_ep, held),
+        (line, held),
+        (line, held),
+        (held,),
+        (held,),
+    ]
+    counts = [n_ep, n_ep, n_ep, n_ep, line, line, line, line, 2, 2]
+    return [pltpu.VMEM(s + (feature,), BF) for s in shapes] + [
+        pltpu.SemaphoreType.DMA((c,)) for c in counts
+    ]
+
+
+def reduce_kernel(n_ep, inp, out, *scratch):
+    at = Spot(n_ep, out.shape[1])
+    job = Reduce(at, inp, out, scratch[:8], scratch[8:])
+    job.start()
+    job.run()
+    job.finish()
+
+
+def reduce_blocks(inp, n_ep, tag):
+    halves, width, feature = inp.shape
+    height = width // n_ep
+    return pl.pallas_call(
+        functools.partial(reduce_kernel, n_ep),
+        out_shape=jax.ShapeDtypeStruct((halves, height, feature), inp.dtype),
+        in_specs=[pl.BlockSpec(memory_space=pltpu.VMEM)],
+        out_specs=pl.BlockSpec(memory_space=pltpu.VMEM),
+        scratch_shapes=reduce_bufs(n_ep, height, feature),
+        compiler_params=pltpu.CompilerParams(collective_id=tag, has_side_effects=True),
+        name=f"reduce_{tag}",
+    )(inp)
+
 
 def dequant(quant, scale):
     shaped = quant.astype(F32).reshape(quant.shape[0], quant.shape[1], -1, QBLOCK)
@@ -32,10 +392,8 @@
     experts, rows_here = route.shape
     count, width = tokens.shape
     feature = cotangent.shape[2]
-    owned = weight.shape[1]
-    piece = owned // n_rep
     total_rows = rows_here * n_rep * n_ep
-    whole = lax.all_gather(weight.astype(BF), "ep", axis=1, tiled=True)
+    whole = gather_blocks(weight.astype(BF), n_ep, 1)
     spots = lax.broadcasted_iota(jnp.int32, (experts, count, rows_here), 1)
     pick = (spots == route[:, None, :]).astype(BF)
     cot = jnp.einsum("etr,erf->etf", pick, cotangent, preferred_element_type=F32)
@@ -43,20 +401,12 @@
     sig = jax.nn.sigmoid(gate)
     dgate = (cot * sig * (1.0 + gate * (1.0 - sig))).astype(BF)
     partial = jnp.einsum("td,etf->edf", tokens, dgate, preferred_element_type=F32).astype(BF)
-    shuffled = (
-        partial.reshape(experts, n_ep, n_rep, piece, feature)
-        .transpose(2, 1, 3, 0, 4)
-        .reshape(n_rep * n_ep * piece, experts * feature)
-    )
-    quarter = lax.psum_scatter(shuffled, "rep", scatter_dimension=0, tiled=True)
-    summed = lax.psum_scatter(quarter, "ep", scatter_dimension=0, tiled=True)
+    grad = reduce_blocks(partial, n_ep, 2).astype(F32) / total_rows
     token_grad = jnp.einsum("etf,edf->td", dgate, whole, preferred_element_type=F32).astype(BF)
-    grad = lax.all_gather(summed, "rep", axis=0, tiled=True).astype(F32)
-    grad = grad.reshape(owned, experts, feature).transpose(1, 0, 2) / total_rows
     step_dir, new_weight = adam_update(
         weight, grad, first_q, first_scale, second_q, second_scale
     )
-    new_whole = lax.all_gather(new_weight.astype(BF), "ep", axis=1, tiled=True)
+    new_whole = gather_blocks(new_weight.astype(BF), n_ep, 3)
     nexts = jnp.einsum("td,edf->etf", tokens, new_whole, preferred_element_type=F32).astype(BF)
     next_gate = jnp.einsum("etr,etf->erf", pick, nexts, preferred_element_type=F32).astype(BF)
     return (token_grad, step_dir, new_weight, next_gate)

time: 341 us -> 155 us (0.45)
  waiting for transfers between devices: 239 us -> 0 us
  Pallas kernels: 0 us -> 107 us
  local copies, waits for them, and re-layouts: 39.2 us -> 9.87 us
  between operations: 13.8 us -> 0.74 us
  blocking collectives: 7.38 us -> 0 us
    all_gather x2 -> x0, waiting for transfers between devices: 133 us -> none  [the longest x1 73.3 us: on_device(): whole = lax.all_gather(weight.astype(BF), 'ep', axis=1, tiled=True)]
    pallas_call x0 -> x3, Pallas kernels: none -> 107 us  [the longest x2 67.5 us: gather_blocks(): pl.pallas_call(functools.partial(gather_kernel, n_ep), out_shape=jax.Shap...]
    reduce_scatter x2 -> x0, waiting for transfers between devices: 105 us -> none  [the longest x1 62.2 us: on_device(): summed = lax.psum_scatter(quarter, 'ep', scatter_dimension=0, tiled=True)]
    unnamed x16, local copies, waits for them, and re-layouts: 19.4 us -> 1.48 us
    transpose x1 -> x0, local copies, waits for them, and re-layouts: 8.51 us -> none  [on_device(): shuffled = partial.reshape(experts, n_ep, n_rep, piece, feature).transpos...]
    all_gather x1 -> x0, blocking collectives: 7.38 us -> none  [on_device(): grad = lax.all_gather(summed, 'rep', axis=0, tiled=True).astype(F32)]
    convert_element_type x1 -> x0, local copies, waits for them, and re-layouts: 6.25 us -> none  [on_device(): jnp.einsum('td,etf->edf', tokens, dgate, preferred_element_type=F32)]
    mul x2 -> x4, local copies, waits for them, and re-layouts: 5.06 us -> 8.39 us  [dequant(): return (shaped * scale[..., None]).reshape(quant.shape)]
  transfers between devices with their start and end apart: 4 -> 0, of which waited for: 4 -> 0; matrix products, arithmetic and copies ran while one was open for 6% -> 0% of each run, Pallas kernels for 0% -> 0%
where the time goes in v2:
time: 155 us
  Pallas kernels  107 us (69%)
  matrix products  31.4 us (20%)
  local copies, waits for them, and re-layouts  9.87 us (6%)
  other arithmetic  5.93 us (4%)
    pallas_call x2, Pallas kernels, gather_blocks(): pl.pallas_call(functools.partial(gather_kernel, n_ep), out_shape=jax.Shap...  67.5 us
    pallas_call x1, Pallas kernels, reduce_blocks(): pl.pallas_call(functools.partial(reduce_kernel, n_ep), out_shape=jax.Shap...  39.5 us
    dot_general x1, matrix products, on_device(): jnp.einsum('etr,etf->erf', pick, nexts, preferred_element_type=F32)  8.67 us
    mul x4, local copies, waits for them, and re-layouts, dequant(): return (shaped * scale[..., None]).reshape(quant.shape)  8.39 us
    dot_general x1, matrix products, on_device(): gate = jnp.einsum('td,edf->etf', tokens, whole, preferred_element_type=F32)  7.14 us
    dot_general x1, matrix products, on_device(): jnp.einsum('td,etf->edf', tokens, dgate, preferred_element_type=F32)  6.42 us
    convert_element_type x1, other arithmetic, on_device(): new_whole = gather_blocks(new_weight.astype(BF), n_ep, 3)  5.07 us
    dot_general x1, matrix products, on_device(): jnp.einsum('etf,edf->td', dgate, whole, preferred_element_type=F32)  4.8 us

profile of v2, /device:TPU:0, one launch (start us, length us, event | category | flops | bytes accessed | tf_op | source)
XLA Modules:
  0.0 154.9 jit_solution(17146265430931823475)
XLA Ops:
  0.6 0.0 copy-start
  0.6 0.0 copy-start.2
  0.7 4.4 %fusion.12 = f32[2,768,512]{2,1,0:T(8,128)} fusion(bf16[2,512,512]{2,1,0:T(8,128)(2,1)} %param.10, s32[2,512]{1,0:T(2,128)} %param.9), kind=kOutput, calls=%fused_computation.17 | convolution fusion | flops 806092800 | bytes 4198400 | tf_op jit(solution)/shard_map/etr,erf->etf/dot_general | solution.py:399
  5.0 0.0 copy-done.2
  5.0 0.9 convert_element_type.34.own
  5.9 34.2 %gather_1.1 = bf16[2,2048,512]{2,1,0:T(8,128)(2,1)} custom-call(bf16[2,256,512]{2,1,0:T(8,128)(2,1)} %convert_element_type.34.own), custom_call_target="tpu_custom_call" | custom-call | tf_op jit(solution)/shard_map/gather_1/pallas_call | solution.py:170
  40.1 0.0 copy-done
  40.1 0.0 copy-start.1
  40.1 7.1 %fusion.5 = bf16[2,768,512]{2,1,0:T(8,128)(2,1)S(1)} fusion(f32[2,768,512]{2,1,0:T(8,128)} %fusion.12, bf16[2,2048,512]{2,1,0:T(8,128)(2,1)} %gather_1.1, bf16[768,2048]{1,0:T(8,128)(2,1)S(1)} %copy-done), kind=kOutput, calls=%fused_computation.9 | convolution fusion | flops 3228303360 | bytes 12058624 | tf_op jit(solution)/shard_map/td,edf->etf/dot_general | solution.py:400
  47.2 0.0 copy-start.6
  47.2 1.2 copy-done.6
  48.4 4.8 %bitcast_convert_fusion = bf16[768,2048]{1,0:T(8,128)(2,1)} fusion(bf16[2,768,512]{2,1,0:T(8,128)(2,1)S(1)} %fusion.5, bf16[2,2048,512]{2,1,0:T(8,128)(2,1)S(1)} %copy-done.1), kind=kOutput, calls=%fused_computation | convolution fusion | flops 3222798336 | bytes 8912896 | tf_op jit(solution)/shard_map/etf,edf->td/dot_general | solution.py:405
  53.2 0.1 copy.18
  53.4 1.6 %mul.74 = f32[2,256,4,128]{3,2,1,0:T(4,128)} broadcast(f32[2,256,4]{2,1,0:T(8,128)S(1)} %copy.18), dimensions={0,1,2} | broadcast | bytes 1056768 | tf_op jit(solution)/shard_map/mul | solution.py:379
  54.9 2.6 %mul.75 = f32[2,256,512]{2,1,0:T(8,128)} reshape(f32[2,256,4,128]{3,2,1,0:T(4,128)} %mul.74) | data formatting | bytes 2097152 | tf_op jit(solution)/shard_map/mul | solution.py:379
  57.6 6.4 %convert_bitcast_fusion.inp = bf16[2,2048,512]{2,1,0:T(8,128)(2,1)} fusion(bf16[2,768,512]{2,1,0:T(8,128)(2,1)} %copy-done.6, bf16[768,2048]{1,0:T(8,128)(2,1)S(1)} %copy-done), kind=kOutput, calls=%fused_computation.1 | convolution fusion | flops 3223322624 | bytes 8912896 | tf_op jit(solution)/shard_map/td,etf->edf/dot_general | solution.py:403
  64.0 39.5 %reduce_2.1 = bf16[2,256,512]{2,1,0:T(8,128)(2,1)} custom-call(bf16[2,2048,512]{2,1,0:T(8,128)(2,1)} %convert_bitcast_fusion.inp), custom_call_target="tpu_custom_call" | custom-call | tf_op jit(solution)/shard_map/reduce_2/pallas_call | solution.py:366
  103.5 0.0 copy-done.4
  103.5 0.1 copy.15
  103.7 1.6 %mul.67 = f32[2,256,4,128]{3,2,1,0:T(4,128)} broadcast(f32[2,256,4]{2,1,0:T(8,128)S(1)} %copy.15), dimensions={0,1,2} | broadcast | bytes 1056768 | tf_op jit(solution)/shard_map/mul | solution.py:379
  105.3 2.6 %mul.68 = f32[2,256,512]{2,1,0:T(8,128)} reshape(f32[2,256,4,128]{3,2,1,0:T(4,128)} %mul.67) | data formatting | bytes 2097152 | tf_op jit(solution)/shard_map/mul | solution.py:379
  107.9 5.1 %fusion.31 = (bf16[2,256,512]{2,1,0:T(8,128)(2,1)}, f32[2,256,512]{2,1,0:T(8,128)}, f32[2,256,512]{2,1,0:T(8,128)}) fusion(f32[2,256,512]{2,1,0:T(8,128)} %param.11, f32[2,256,512]{2,1,0:T(8,128)} %mul.75, s32[2,256,512]{2,1,0:T(8,128)} %param.14, bf16[2,256,512]{2,1,0:T(8,128)(2,1)} %reduce_2.1, f32[2,256,512]{2,1,0:T(8,128)} %mul.68, s32[2,256,512]{2,1,0:T(8,128)} %param.12), kind=kLoop, calls=%fused_computation.34 | loop fusion | flops 5242880 | bytes 8388608 | tf_op jit(solution)/shard_map/convert_element_type | solution.py:409
  112.9 33.3 %gather_3.1 = bf16[2,2048,512]{2,1,0:T(8,128)(2,1)} custom-call(bf16[2,256,512]{2,1,0:T(8,128)(2,1)} %get-tuple-element.4.own), custom_call_target="tpu_custom_call" | custom-call | tf_op jit(solution)/shard_map/gather_3/pallas_call | solution.py:170
  146.3 8.7 %fusion.20 = bf16[2,512,512]{2,1,0:T(8,128)(2,1)} fusion(s32[2,512]{1,0:T(2,128)S(1)} %copy-done.5, bf16[2,2048,512]{2,1,0:T(8,128)(2,1)} %gather_3.1, bf16[768,2048]{1,0:T(8,128)(2,1)S(1)} %copy-done), kind=kOutput, calls=%fused_computation.24 | convolution fusion | flops 4028628992 | bytes 8392704 | tf_op jit(solution)/shard_map/etr,etf->erf/dot_general | solution.py:411
  (6 shorter events, 0.0 us)
Async XLA Ops:
  0.6 39.4 %copy-start = (bf16[768,2048]{1,0:T(8,128)(2,1)S(1)}, bf16[768,2048]{1,0:T(8,128)(2,1)}, u32[]{:S(2)}) copy-start(bf16[768,2048]{1,0:T(8,128)(2,1)} %param.8) | copy-start | bytes 9437188
  0.6 4.4 %copy-start.2 = (f32[2,256,512]{2,1,0:T(8,128)S(1)}, f32[2,256,512]{2,1,0:T(8,128)}, u32[]{:S(2)}) copy-start(f32[2,256,512]{2,1,0:T(8,128)} %param.11) | copy-start | bytes 3145732
  40.1 8.3 %copy-start.1 = (bf16[2,2048,512]{2,1,0:T(8,128)(2,1)S(1)}, bf16[2,2048,512]{2,1,0:T(8,128)(2,1)}, u32[]{:S(2)}) copy-start(bf16[2,2048,512]{2,1,0:T(8,128)(2,1)} %gather_1.1) | copy-start | bytes 12582916
  47.2 1.2 copy-start.6
  48.4 4.8 %copy-start.3 = (f32[2,256,4]{1,2,0:T(4,128)S(1)}, f32[2,256,4]{1,2,0:T(4,128)}, u32[]{:S(2)}) copy-start(f32[2,256,4]{1,2,0:T(4,128)} %param.15) | copy-start | bytes 24580
  64.0 39.5 %copy-start.4 = (f32[2,256,4]{1,2,0:T(4,128)S(1)}, f32[2,256,4]{1,2,0:T(4,128)}, u32[]{:S(2)}) copy-start(f32[2,256,4]{1,2,0:T(4,128)} %param.13) | copy-start | bytes 24580
  112.9 33.3 %copy-start.5 = (s32[2,512]{1,0:T(2,128)S(1)}, s32[2,512]{1,0:T(2,128)}, u32[]{:S(2)}) copy-start(s32[2,512]{1,0:T(2,128)} %param.9) | copy-start | bytes 12292

commit v3 on v2

v3 whole, which is shorter than its diff:
```python
import functools

import jax
import jax.numpy as jnp
from jax import lax
from jax.experimental import pallas as pl
from jax.experimental.pallas import tpu as pltpu
from jax.sharding import PartitionSpec as P

QBLOCK = 128
BETA_ONE = 0.9
BETA_TWO = 0.95
CORR_ONE = 1.0 - 0.9**10
CORR_TWO = 1.0 - 0.95**10
EPSILON = 1e-08
RATE = 0.002
BF = jnp.bfloat16
F32 = jnp.float32

MESH = pl.DeviceIdType.MESH
TILE = 16


class Spot:
    def __init__(self, n_ep, height):
        self.rep, self.ep = lax.axis_index("rep"), lax.axis_index("ep")
        self.core, self.y = self.rep % 2, self.rep // 2
        self.x, self.z = self.ep % 2, self.ep // 2
        self.n_ep, self.line, self.height = n_ep, n_ep // 2, height
        self.alone = height // TILE * 3 // 8 * TILE
        self.held = height - self.alone
        self.both = self.held - self.alone
        self.start = self.y * self.alone
        self.x_peer = (self.rep, self.z * 2 + 1 - self.x)
        self.y_peer = ((1 - self.y) * 2 + self.core, self.ep)
        self.core_peer = (self.y * 2 + 1 - self.core, self.ep)
        self.order = []
        for k in range(1, self.line // 2 + 1):
            self.order += [k] if k == self.line - k else [k, self.line - k]

    def near(self, j):
        last = self.line - 1
        few = jnp.where(2 * self.z < last, self.z, last - self.z)
        far = jnp.where(2 * self.z < last, 1, -1)
        sign = jnp.where(j < 2 * few, 1 - 2 * (j % 2), far)
        return self.z + sign * jnp.where(j < 2 * few, j // 2 + 1, j - few + 1), sign

    def z_peer(self, k):
        return (self.rep, (self.z + k) % self.line * 2 + self.x)

    def meet(self):
        barrier = pltpu.get_barrier_semaphore()
        peers = [self.z_peer(k) for k in range(1, self.line)]
        peers += [self.x_peer, self.y_peer, self.core_peer]
        for peer in peers:
            pl.semaphore_signal(barrier, inc=1, device_id=peer, device_id_type=MESH)
        pl.semaphore_wait(barrier, len(peers))


def tiled(value):
    return pl.multiple_of(value, TILE)


def remote(src, dst, send, recv, peer):
    return pltpu.make_async_remote_copy(
        src_ref=src, dst_ref=dst, send_sem=send, recv_sem=recv, device_id=peer, device_id_type=MESH
    )


class Gather:
    def __init__(self, at, own, out, sems):
        self.at, self.own, self.out = at, own, out
        (self.zs, self.xs, self.ys, self.c1s, self.c2s, self.r1, self.r2, self.r3, self.r4) = sems

    def part(self, half, ep, first, rows):
        return self.out.at[half, pl.ds(tiled(ep * self.at.height + first), rows)]

    def mine(self, ep):
        return self.part(self.at.core, ep, self.at.start, self.at.held)

    def first_copies(self, act):
        at = self.at
        src = self.own.at[at.core, pl.ds(tiled(at.start), at.held)]

        def to(sem, peer):
            return remote(src, self.mine(at.ep), sem, self.r1.at[at.ep], peer)

        @pl.when(at.z + 1 < at.line)
        def _():
            act(to(self.zs.at[at.line - 1], at.z_peer(1)))

        @pl.when(at.z > 0)
        def _():
            act(to(self.zs.at[at.line], at.z_peer(at.line - 1)))

        act(to(self.xs.at[at.line - 1], at.x_peer))

    def line_copies(self, j, act):
        at = self.at
        z, sign = at.near(j)
        ep = z * 2 + at.x
        rows = self.mine(ep)
        onward = at.z - sign

        @pl.when((onward >= 0) & (onward < at.line))
        def _():
            peer = (at.rep, onward * 2 + at.x)
            act(remote(rows, rows, self.zs.at[j], self.r1.at[ep], peer))

        act(remote(rows, rows, self.xs.at[j], self.r1.at[ep], at.x_peer))

    def share_copies(self, ep, act):
        at = self.at
        if at.alone:
            rows = self.part(at.core, ep, at.y * at.held, at.alone)
            act(remote(rows, rows, self.ys.at[ep], self.r2.at[ep], at.y_peer))
        act(remote(self.mine(ep), self.mine(ep), self.c1s.at[ep], self.r3.at[ep], at.core_peer))

    def late_copy(self, ep):
        at = self.at
        rows = self.part(at.core, ep, (1 - at.y) * at.held, at.alone)
        return remote(rows, rows, self.c2s.at[ep], self.r4.at[ep], at.core_peer)

    def arrive(self, dst, recv):
        remote(dst, dst, self.zs.at[0], recv, self.at.x_peer).wait_recv()

    def start(self):
        self.first_copies(lambda copy: copy.start())

    def from_line(self, j):
        at = self.at
        ep = at.near(j)[0] * 2 + at.x
        self.arrive(self.mine(ep), self.r1.at[ep])
        self.line_copies(j, lambda copy: copy.start())
        self.share_copies(ep, lambda copy: copy.start())
        return ep

    def from_pair(self, j):
        at = self.at
        ep = (at.z if j < 0 else at.near(j)[0]) * 2 + 1 - at.x
        self.arrive(self.mine(ep), self.r1.at[ep])
        self.share_copies(ep, lambda copy: copy.start())
        return ep

    def late(self, ep):
        at = self.at
        if at.alone:
            rows = self.part(at.core, ep, (1 - at.y) * at.held, at.alone)
            self.arrive(rows, self.r2.at[ep])
            self.late_copy(ep).start()

    def whole(self, ep):
        at = self.at
        self.arrive(self.part(1 - at.core, ep, at.start, at.held), self.r3.at[ep])
        if at.alone:
            rows = self.part(1 - at.core, ep, (1 - at.y) * at.held, at.alone)
            self.arrive(rows, self.r4.at[ep])

    def relay(self, tasks, use):
        at = self.at
        tasks = list(tasks)
        order = []
        for j in range(at.line - 1):
            for step, k in ((self.from_line, j), (self.from_pair, j - 1)):
                order.append(step(k))
                if tasks:
                    tasks.pop(0)()
        order.append(self.from_pair(at.line - 2))
        for task in tasks:
            task()
        behind = None
        for ep in order:
            self.late(ep)
            if behind is not None:
                self.whole(behind)
                use(behind)
            behind = ep
        self.whole(behind)
        use(behind)

    def end(self):
        at = self.at

        def done(copy):
            copy.wait_send()

        self.first_copies(done)
        for j in range(at.line - 1):
            self.line_copies(j, done)

        @pl.loop(1, at.n_ep)
        def _(k):
            ep = (at.ep + k) % at.n_ep
            self.share_copies(ep, done)
            if at.alone:
                self.late_copy(ep).wait_send()


def gather_sems(n_ep):
    line = n_ep // 2
    return [pltpu.SemaphoreType.DMA((line + 1,)), pltpu.SemaphoreType.DMA((line,))] + [
        pltpu.SemaphoreType.DMA((n_ep,)) for _ in range(7)
    ]


class Reduce:
    def __init__(self, at, term, fill, inp, out, bufs, sems):
        self.at, self.term, self.fill, self.inp, self.out = at, term, fill, inp, out
        (self.bc, self.s1, self.by, self.s2, self.bx, self.bz, self.fin, self.by2) = bufs
        (self.cs, self.cr, self.ys, self.yr, self.xs, self.xr, self.zs, self.zr, self.fs, self.fr) = sems

    def block(self, i):
        at = self.at
        far = jnp.where(i < at.line, 1, 0)
        z = (at.z + 1 + i) % at.line
        x = at.x + far - 2 * at.x * far
        return z, z * 2 + x

    def core_copy(self, ep):
        at = self.at
        return remote(
            self.inp.at[1 - at.core, pl.ds(tiled(ep * at.height), at.height)],
            self.bc.at[ep],
            self.cs.at[ep],
            self.cr.at[ep],
            at.core_peer,
        )

    def y_copy(self, ep):
        at = self.at
        return remote(
            self.s1.at[ep, pl.ds(tiled((1 - at.y) * at.held), at.alone)],
            self.by.at[ep],
            self.ys.at[ep],
            self.yr.at[ep],
            at.y_peer,
        )

    def x_copy(self, z, ep):
        return remote(self.s2.at[ep], self.bx.at[z], self.xs.at[z], self.xr.at[z], self.at.x_peer)

    def z_copy(self, k, ep):
        at = self.at
        return remote(self.s2.at[ep], self.bz.at[k], self.zs.at[k], self.zr.at[k], at.z_peer(k))

    def first(self, i):
        at = self.at
        _, ep = self.block(i)
        self.core_copy(ep).wait_recv()
        here = self.inp[at.core, pl.ds(tiled(ep * at.height), at.height)].astype(F32)
        self.s1[ep] = (here + self.bc[ep].astype(F32)).astype(BF)
        if at.alone:
            self.y_copy(ep).start()

    def pieces(self, ep):
        at = self.at
        found = []
        if at.alone:
            self.y_copy(ep).wait_recv()
            value = self.s1[ep, pl.ds(tiled(at.y * at.held), at.alone)].astype(F32)
            found.append((tiled(at.y * at.both), at.alone, value + self.by[ep].astype(F32)))
        value = self.s1[ep, pl.ds(at.alone, at.both)].astype(F32)
        found.append((tiled((1 - at.y) * at.alone), at.both, value))
        return found

    def second_far(self, i):
        z, ep = self.block(i)
        for first, rows, value in self.pieces(ep):
            self.s2[ep, pl.ds(first, rows)] = value.astype(BF)
        self.x_copy(z, ep).start()

    def second_near(self, i):
        z, ep = self.block(i)
        found = self.pieces(ep)
        self.x_copy(z, ep).wait_recv()
        for first, rows, value in found:
            total = value + self.bx[z, pl.ds(first, rows)].astype(F32)
            self.s2[ep, pl.ds(first, rows)] = total.astype(BF)

    def make(self, i):
        at = self.at
        _, ep = self.block(i)
        rows = pl.ds(tiled(ep * at.height), at.height)
        self.inp[1 - at.core, rows] = self.term(1 - at.core, rows).astype(BF)
        self.core_copy(ep).start()
        self.inp[at.core, rows] = self.term(at.core, rows).astype(BF)

    def ahead(self, i, lag):
        @pl.when(i + 2 * lag < self.at.n_ep)
        def _():
            self.make(i + 2 * lag)

        @pl.when(i + lag < self.at.n_ep)
        def _():
            self.first(i + lag)

    def run(self, lag=2):
        at = self.at
        self.make(0)
        for i in range(lag):
            for j in range(2 * i + 1, min(2 * i + 3, 2 * lag)):
                self.make(j)
            self.first(i)

        @pl.loop(0, at.line)
        def _(i):
            self.ahead(i, lag)
            self.second_far(i)
            self.fill(i)

        @pl.loop(at.line, at.n_ep - 1)
        def _(i):
            self.ahead(i, lag)
            self.second_near(i)
            k = i - at.line + 1
            _, ep = self.block(i)
            self.z_copy(k, ep).start()
            self.fill(i)

        self.second_near(at.n_ep - 1)
        self.fill(at.n_ep - 1)

    def finish(self):
        at = self.at
        total = self.s2[at.ep].astype(F32)
        for k in range(1, at.line):
            self.z_copy(k, at.ep).wait_recv()
            total += self.bz[k].astype(F32)
        self.fin[...] = total.astype(BF)
        swap = remote(self.fin, self.by2, self.fs.at[0], self.fr.at[0], at.y_peer)
        swap.start()
        half = self.out.at[at.core]
        if at.alone:
            half[pl.ds(tiled(at.y * at.held), at.alone)] = self.fin[
                pl.ds(tiled(at.y * at.both), at.alone)
            ]
        swap.wait()
        if at.alone:
            half[pl.ds(tiled((1 - at.y) * at.held), at.alone)] = self.by2[
                pl.ds(tiled((1 - at.y) * at.both), at.alone)
            ]
        here = self.fin[pl.ds(tiled((1 - at.y) * at.alone), at.both)].astype(F32)
        there = self.by2[pl.ds(tiled(at.y * at.alone), at.both)].astype(F32)
        half[pl.ds(at.alone, at.both)] = (here + there).astype(BF)
        last = remote(half, half, self.fs.at[1], self.fr.at[1], at.core_peer)
        last.start()
        last.wait_send()
        other = self.out.at[1 - at.core]
        remote(other, other, self.fs.at[1], self.fr.at[1], at.core_peer).wait_recv()

        @pl.loop(0, at.n_ep)
        def _(i):
            _, ep = self.block(i)
            self.core_copy(ep).wait_send()
            if at.alone:
                self.y_copy(ep).wait_send()

        @pl.loop(0, at.line)
        def _(i):
            z, ep = self.block(i)
            self.x_copy(z, ep).wait_send()

        @pl.loop(1, at.line)
        def _(k):
            self.z_copy(k, at.ep).wait_send()


def reduce_bufs(n_ep, height, feature):
    line = n_ep // 2
    alone = height // TILE * 3 // 8 * TILE
    held = height - alone
    shapes = [
        (n_ep, height),
        (n_ep, height),
        (n_ep, max(alone, TILE)),
        (n_ep, held),
        (line, held),
        (line, held),
        (held,),
        (held,),
    ]
    counts = [n_ep, n_ep, n_ep, n_ep, line, line, line, line, 2, 2]
    return [pltpu.VMEM(s + (feature,), BF) for s in shapes] + [
        pltpu.SemaphoreType.DMA((c,)) for c in counts
    ]


CHUNK = 256
LANES = 128


def dot(a, b, dims=((1,), (0,))):
    return lax.dot_general(a, b, (dims, ((), ())), preferred_element_type=F32)


def step_kernel(n_ep, total_rows, *refs):
    (tokens, route, cot, own, weight, fq, fs, sq, ss) = refs[:9]
    (token_grad, step_dir, new_weight, next_gate) = refs[9:13]
    (pick, pick_t, tok_t, spread, acc, dgate, whole, again, inp, grad, own_b) = refs[13:24]
    bufs, sems = refs[24:32], refs[32:42]
    sems_one, sems_two = refs[42:51], refs[51:60]
    halves, height, feature = own.shape
    count, width = tokens.shape
    picked = route.shape[1]
    at = Spot(n_ep, height)
    by_block = height % LANES == 0

    def tiles(extent, body):
        size = CHUNK if extent % CHUNK == 0 else extent

        @pl.loop(0, extent // size)
        def _(t):
            body(pl.ds(pl.multiple_of(t * size, size), size))

    def project(half, cols, matrix, brows, fresh):
        def body(rows):
            value = dot(tokens[rows, cols], matrix[half, brows])
            acc[half, rows] = value if fresh else acc[half, rows] + value

        tiles(count, body)

    def use_block(matrix, ep, fresh=False):
        if by_block:
            spot = pl.ds(pl.multiple_of(ep * height, height), height)
            for half in range(halves):
                project(half, spot, matrix, spot, fresh)

    def use_rest(matrix):
        if not by_block:
            for half in range(halves):
                for j in range(width // CHUNK):
                    spot = pl.ds(j * CHUNK, CHUNK)
                    project(half, spot, matrix, spot, j == 0)

    def scatter(half):
        def body(rows):
            spots = lax.broadcasted_iota(jnp.int32, (rows.size, picked), 0) + rows.start
            hits = (spots == route[pl.ds(half, 1), :]).astype(F32).astype(BF)
            pick[half, rows] = hits
            spread[half, rows] = dot(hits, cot[half]).astype(BF)

        tiles(count, body)

    def flip_pick(half):
        pick_t[half] = pick[half].T

    def flip(j):
        spot = pl.ds(j * CHUNK, CHUNK)
        tok_t[spot, :] = tokens[:, spot].T

    def both(task, *args):
        for half in range(halves):
            task(half)

    own_rows = pl.ds(tiled(at.ep * height), height)
    one = Gather(at, own, whole, sems_one)
    at.meet()
    one.start()
    whole[:, own_rows] = own[...]
    flips = [functools.partial(flip, j) for j in range(width // CHUNK)]
    tasks = [functools.partial(scatter, h) for h in range(halves)]
    tasks.insert(1, lambda: use_block(whole, at.ep, True))
    tasks += [functools.partial(flip_pick, h) for h in range(halves)]
    while flips:
        pair = flips[:4]
        flips = flips[4:]
        tasks.append(lambda pair=pair: [f() for f in pair])
    one.relay(tasks, lambda ep: use_block(whole, ep))
    use_rest(whole)

    for half in range(halves):

        def shape_grad(rows):
            gate = acc[half, rows]
            sig = 1.0 / (1.0 + jnp.exp(-gate))
            value = spread[half, rows].astype(F32) * sig * (1.0 + gate * (1.0 - sig))
            dgate[half, rows] = value.astype(BF)

        tiles(count, shape_grad)

    def term(half, rows):
        return dot(tok_t[rows, :], dgate[half])

    def back(j):
        @pl.when(j < width // CHUNK)
        def _():
            spot = pl.ds(pl.multiple_of(j * CHUNK, CHUNK), CHUNK)

            def body(rows):
                value = dot(dgate[0, rows], whole[0, spot], ((1,), (1,)))
                for half in range(1, halves):
                    value += dot(dgate[half, rows], whole[half, spot], ((1,), (1,)))
                token_grad[rows, spot] = value.astype(BF)

            tiles(count, body)

    job = Reduce(at, term, back, inp, grad, bufs, sems)
    job.run()
    for j in range(n_ep, width // CHUNK):
        back(j)
    job.finish()

    slab = 64 if height % 64 == 0 else height
    for half in range(halves):

        @pl.loop(0, height // slab)
        def _(t):
            rows = pl.ds(pl.multiple_of(t * slab, slab), slab)
            for q in range(feature // QBLOCK):
                cols = pl.ds(q * QBLOCK, QBLOCK)
                here = (half, rows, cols)
                g = grad[here].astype(F32) / total_rows
                first = BETA_ONE * (fq[here].astype(F32) * fs[half, rows, pl.ds(q, 1)])
                second = BETA_TWO * (sq[here].astype(F32) * ss[half, rows, pl.ds(q, 1)])
                first += (1.0 - BETA_ONE) * g
                second += (1.0 - BETA_TWO) * g * g
                step = first / CORR_ONE / (jnp.sqrt(second / CORR_TWO) + EPSILON)
                fresh = weight[here] - RATE * step
                step_dir[here] = step
                new_weight[here] = fresh
                own_b[here] = fresh.astype(BF)

    two = Gather(at, own_b, again, sems_two)
    two.start()
    again[:, own_rows] = own_b[...]
    two.relay([lambda: use_block(again, at.ep, True)], lambda ep: use_block(again, ep))
    use_rest(again)
    for half in range(halves):
        rounded = acc[half].astype(BF)

        def put(rows):
            next_gate[half, rows] = dot(pick_t[half, rows], rounded).astype(BF)

        tiles(picked, put)
    one.end()
    two.end()


def on_device(tokens, route, cotangent, weight, first_q, first_scale, second_q, second_scale):
    n_rep = lax.axis_size("rep")
    n_ep = lax.axis_size("ep")
    halves, picked = route.shape
    count, width = tokens.shape
    feature = cotangent.shape[2]
    height = weight.shape[1]
    total_rows = picked * n_rep * n_ep
    vmem = pltpu.VMEM
    scratch = [
        vmem((halves, count, picked), BF),
        vmem((halves, picked, count), BF),
        vmem((width, count), BF),
        vmem((halves, count, feature), BF),
        vmem((halves, count, feature), F32),
        vmem((halves, count, feature), BF),
        vmem((halves, width, feature), BF),
        vmem((halves, width, feature), BF),
        vmem((halves, width, feature), BF),
        vmem((halves, height, feature), BF),
        vmem((halves, height, feature), BF),
    ]
    scratch += reduce_bufs(n_ep, height, feature) + gather_sems(n_ep) + gather_sems(n_ep)
    in_vmem = pl.BlockSpec(memory_space=pltpu.VMEM)
    return pl.pallas_call(
        functools.partial(step_kernel, n_ep, total_rows),
        out_shape=(
            jax.ShapeDtypeStruct(tokens.shape, BF),
            jax.ShapeDtypeStruct(weight.shape, F32),
            jax.ShapeDtypeStruct(weight.shape, F32),
            jax.ShapeDtypeStruct(cotangent.shape, BF),
        ),
        in_specs=[in_vmem] * 9,
        out_specs=(in_vmem,) * 4,
        scratch_shapes=scratch,
        compiler_params=pltpu.CompilerParams(
            collective_id=1, has_side_effects=True, vmem_limit_bytes=62 << 20
        ),
        name="hot_step",
    )(
        tokens, route, cotangent, weight.astype(BF),
        weight, first_q, first_scale, second_q, second_scale,
    )


def solution(mesh):
    in_specs = (
        P(("rep", "ep"), None),
        P(None, ("rep", "ep")),
        P(None, ("rep", "ep"), None),
        P(None, "ep", None),
        P(None, "ep", None),
        P(None, "ep", None),
        P(None, "ep", None),
        P(None, "ep", None),
    )
    out_specs = (
        P(("rep", "ep"), None),
        P(None, "ep", None),
        P(None, "ep", None),
        P(None, ("rep", "ep"), None),
    )
    return jax.shard_map(
        on_device, mesh=mesh, in_specs=in_specs, out_specs=out_specs, check_vma=False
    )
```

time: 155 us -> 125 us (0.81)
  matrix products: 31.4 us -> 0 us
  Pallas kernels: 107 us -> 112 us
  other arithmetic: 5.93 us -> 2.08 us
    dot_general x5 -> x0, matrix products: 31.4 us -> none  [the longest x1 8.67 us: on_device(): jnp.einsum('etr,etf->erf', pick, nexts, preferred_element_type=F32)]
    unnamed x16 -> x12, local copies, waits for them, and re-layouts: 1.48 us -> 10.1 us
    mul x4 -> x0, local copies, waits for them, and re-layouts: 8.39 us -> none  [dequant(): return (shaped * scale[..., None]).reshape(quant.shape)]
    pallas_call x3 -> x1, Pallas kernels: 107 us -> 112 us  [on_device(): pl.pallas_call(functools.partial(step_kernel, n_ep, total_rows), out_shap...]
    convert_element_type x2 -> x1, other arithmetic: 5.93 us -> 2.08 us  [on_device(): weight.astype(BF)]
where the time goes in v3:
time: 125 us
  Pallas kernels  112 us (90%)
  local copies, waits for them, and re-layouts  10.1 us (8%)
  other arithmetic  2.08 us (2%)
    pallas_call x1, Pallas kernels, on_device(): pl.pallas_call(functools.partial(step_kernel, n_ep, total_rows), out_shap...  112 us
    unnamed x12, local copies, waits for them, and re-layouts  10.1 us

profile of v3, /device:TPU:0, one launch (start us, length us, event | category | flops | bytes accessed | tf_op | source)
XLA Modules:
  0.0 125.1 jit_solution(12837292745765676683)
XLA Ops:
  0.6 1.6 %copy.12.refs_6_ = f32[2,256,4]{2,1,0:T(8,128)} copy(f32[2,256,4]{1,2,0:T(4,128)} %param.13) | data formatting | bytes 16384 | tf_op args[5]
  2.2 1.5 %copy.13.refs_8_ = f32[2,256,4]{2,1,0:T(8,128)} copy(f32[2,256,4]{1,2,0:T(4,128)} %param.15) | data formatting | bytes 16384 | tf_op args[7]
  3.7 2.1 %convert_element_type.3.refs_3_ = bf16[2,256,512]{2,1,0:T(8,128)(2,1)} convert(f32[2,256,512]{2,1,0:T(8,128)} %refs_4_.1) | non-fusion elementwise | flops 262144 | bytes 1572864 | tf_op jit(solution)/shard_map/convert_element_type | solution.py:579
  5.8 112.2 %hot_step.1 = (bf16[768,2048]{1,0:T(8,128)(2,1)}, f32[2,256,512]{2,1,0:T(8,128)}, f32[2,256,512]{2,1,0:T(8,128)}, bf16[2,512,512]{2,1,0:T(8,128)(2,1)}) custom-call(bf16[768,2048]{1,0:T(8,128)(2,1)} %refs_0_.1, s32[2,512]{1,0:T(2,128)} %refs_1_.1, bf16[2,512,512]{2,1,0:T(8,128)(2,1)} %refs_2_.1, bf16[2,256,512]{2,1,0:T(8,128)(2,1)} %convert_element_type.3.refs_3_, ...), custom_call_target="tpu_custom_call" | custom-call | tf_op jit(solution)/shard_map/hot_step/pallas_call | solution.py:563
  118.0 0.0 copy-start.2
  118.0 0.0 copy-start.1
  118.0 4.1 %copy.18 = bf16[768,2048]{1,0:T(8,128)(2,1)} copy(bf16[768,2048]{1,0:T(8,128)(2,1)} %get-tuple-element.8) | data formatting | bytes 6291456
  122.2 0.0 copy-done.2
  122.2 0.0 copy-start
  122.2 1.0 copy.19
  123.1 0.0 copy-done.1
  123.1 1.0 copy.20
  124.1 0.0 copy-done
  124.1 1.0 copy.21
Async XLA Ops:
  118.0 4.1 %copy-start.2 = (f32[2,256,512]{2,1,0:T(8,128)S(1)}, f32[2,256,512]{2,1,0:T(8,128)}, u32[]{:S(2)}) copy-start(f32[2,256,512]{2,1,0:T(8,128)} %get-tuple-element.9) | copy-start | bytes 3145732
  118.0 5.1 %copy-start.1 = (f32[2,256,512]{2,1,0:T(8,128)S(1)}, f32[2,256,512]{2,1,0:T(8,128)}, u32[]{:S(2)}) copy-start(f32[2,256,512]{2,1,0:T(8,128)} %get-tuple-element.10) | copy-start | bytes 3145732
  122.2 1.9 %copy-start = (bf16[2,512,512]{2,1,0:T(8,128)(2,1)S(1)}, bf16[2,512,512]{2,1,0:T(8,128)(2,1)}, u32[]{:S(2)}) copy-start(bf16[2,512,512]{2,1,0:T(8,128)(2,1)} %get-tuple-element.11) | copy-start | bytes 3145732

commit v4 on v3

--- a/solution.py
+++ b/solution.py
@@ -394,12 +394,14 @@
 
 
 def step_kernel(n_ep, total_rows, *refs):
-    (tokens, route, cot, own, weight, fq, fs, sq, ss) = refs[:9]
-    (token_grad, step_dir, new_weight, next_gate) = refs[9:13]
-    (pick, pick_t, tok_t, spread, acc, dgate, whole, again, inp, grad, own_b) = refs[13:24]
+    sources = refs[:8]
+    (token_grad, step_dir, new_weight, next_gate) = refs[8:12]
+    (pick, pick_t, tok_t, spread, acc, dgate, whole, again, inp, grad, own, own_b) = refs[12:24]
     bufs, sems = refs[24:32], refs[32:42]
-    sems_one, sems_two = refs[42:51], refs[51:60]
-    halves, height, feature = own.shape
+    sems_one, sems_two, scales = refs[42:51], refs[51:60], refs[60]
+    (tokens, route, cot, weight, fq, fs, sq, ss) = refs[61:69]
+    landed = refs[69]
+    halves, height, feature = weight.shape
     count, width = tokens.shape
     picked = route.shape[1]
     at = Spot(n_ep, height)
@@ -454,9 +456,19 @@
 
     own_rows = pl.ds(tiled(at.ep * height), height)
     one = Gather(at, own, whole, sems_one)
+    loads = [
+        pltpu.make_async_copy(src, dst, landed.at[i])
+        for i, (src, dst) in enumerate(zip(sources, refs[61:69]))
+    ]
+    for i in (3, 1, 2, 0, 4, 5, 6, 7):
+        loads[i].start()
+    loads[3].wait()
+    own[...] = weight[...].astype(BF)
     at.meet()
     one.start()
     whole[:, own_rows] = own[...]
+    for i in (1, 2, 0):
+        loads[i].wait()
     flips = [functools.partial(flip, j) for j in range(width // CHUNK)]
     tasks = [functools.partial(scatter, h) for h in range(halves)]
     tasks.insert(1, lambda: use_block(whole, at.ep, True))
@@ -500,8 +512,12 @@
         back(j)
     job.finish()
 
+    for i in (4, 5, 6, 7):
+        loads[i].wait()
     slab = 64 if height % 64 == 0 else height
     for half in range(halves):
+        scales[0] = fs[half].T
+        scales[1] = ss[half].T
 
         @pl.loop(0, height // slab)
         def _(t):
@@ -510,8 +526,8 @@
                 cols = pl.ds(q * QBLOCK, QBLOCK)
                 here = (half, rows, cols)
                 g = grad[here].astype(F32) / total_rows
-                first = BETA_ONE * (fq[here].astype(F32) * fs[half, rows, pl.ds(q, 1)])
-                second = BETA_TWO * (sq[here].astype(F32) * ss[half, rows, pl.ds(q, 1)])
+                first = BETA_ONE * (fq[here].astype(F32) * scales[0, rows, pl.ds(q, 1)])
+                second = BETA_TWO * (sq[here].astype(F32) * scales[1, rows, pl.ds(q, 1)])
                 first += (1.0 - BETA_ONE) * g
                 second += (1.0 - BETA_TWO) * g * g
                 step = first / CORR_ONE / (jnp.sqrt(second / CORR_TWO) + EPSILON)
@@ -557,8 +573,14 @@
         vmem((halves, width, feature), BF),
         vmem((halves, height, feature), BF),
         vmem((halves, height, feature), BF),
+        vmem((halves, height, feature), BF),
     ]
     scratch += reduce_bufs(n_ep, height, feature) + gather_sems(n_ep) + gather_sems(n_ep)
+    scratch += [vmem((2, height, first_scale.shape[2]), F32)]
+    given = [tokens, route, cotangent, weight, first_q]
+    given += [first_scale.transpose(0, 2, 1), second_q, second_scale.transpose(0, 2, 1)]
+    given = [pltpu.with_memory_space_constraint(a, pltpu.HBM) for a in given]
+    scratch += [vmem(a.shape, a.dtype) for a in given] + [pltpu.SemaphoreType.DMA((8,))]
     in_vmem = pl.BlockSpec(memory_space=pltpu.VMEM)
     return pl.pallas_call(
         functools.partial(step_kernel, n_ep, total_rows),
@@ -568,17 +590,14 @@
             jax.ShapeDtypeStruct(weight.shape, F32),
             jax.ShapeDtypeStruct(cotangent.shape, BF),
         ),
-        in_specs=[in_vmem] * 9,
+        in_specs=[pl.BlockSpec(memory_space=pltpu.HBM)] * 8,
         out_specs=(in_vmem,) * 4,
         scratch_shapes=scratch,
         compiler_params=pltpu.CompilerParams(
-            collective_id=1, has_side_effects=True, vmem_limit_bytes=62 << 20
+            collective_id=1, has_side_effects=True, vmem_limit_bytes=46 << 20
         ),
         name="hot_step",
-    )(
-        tokens, route, cotangent, weight.astype(BF),
-        weight, first_q, first_scale, second_q, second_scale,
-    )
+    )(*given)
 
 
 def solution(mesh):

time: 125 us -> 113 us (0.904)
  local copies, waits for them, and re-layouts: 10.1 us -> 4.58 us
  Pallas kernels: 112 us -> 108 us
  other arithmetic: 2.08 us -> 0 us
    unnamed x12 -> x4, local copies, waits for them, and re-layouts: 10.1 us -> 4.58 us
    pallas_call x1, Pallas kernels: 112 us -> 108 us  [on_device(): pl.pallas_call(functools.partial(step_kernel, n_ep, total_rows), out_shap...]
    convert_element_type x1 -> x0, other arithmetic: 2.08 us -> none  [on_device(): weight.astype(BF)]
where the time goes in v4:
time: 113 us
  Pallas kernels  108 us (96%)
  local copies, waits for them, and re-layouts  4.58 us (4%)
    pallas_call x1, Pallas kernels, on_device(): pl.pallas_call(functools.partial(step_kernel, n_ep, total_rows), out_shap...  108 us
    unnamed x4, local copies, waits for them, and re-layouts  4.58 us

profile of v4, /device:TPU:0, one launch (start us, length us, event | category | flops | bytes accessed | tf_op | source)
XLA Modules:
  0.0 113.0 jit_solution(6066335538459766345)
XLA Ops:
  0.6 107.8 %hot_step.1 = (bf16[768,2048]{1,0:T(8,128)(2,1)S(1)}, f32[2,256,512]{2,1,0:T(8,128)S(1)}, f32[2,256,512]{2,1,0:T(8,128)S(1)}, bf16[2,512,512]{2,1,0:T(8,128)(2,1)S(1)}) custom-call(bf16[768,2048]{1,0:T(8,128)(2,1)} %refs_0_.1, s32[2,512]{1,0:T(2,128)} %refs_1_.1, bf16[2,512,512]{2,1,0:T(8,128)(2,1)} %refs_2_.1, f32[2,256,512]{2,1,0:T(8,128)} %refs_3_.1, ...), custom_call_target="tpu_custom_call" | custom-call | tf_op jit(solution)/shard_map/hot_step/pallas_call | solution.py:585
  108.4 1.7 %copy.16 = bf16[768,2048]{1,0:T(8,128)(2,1)} copy(bf16[768,2048]{1,0:T(8,128)(2,1)S(1)} %get-tuple-element.8) | data formatting | bytes 6291456
  110.1 1.0 copy.17
  111.0 1.0 copy.18
  112.0 1.0 copy.19
